TPU v7x, 32 devices: a whole 2x2x4 slice. The times are simulated.
32 devices in a mesh: tm: 4 (over z), space: 8 (over y, x, core).
Axes of the slice: x: 2, y: 2, z: 4, core: 2. Of those that a mesh axis runs over, the one named last changes fastest.
Arguments:
- thickness: float32 [4, 256, 2048], P('tm', 'space'), may hold values from 0 to 2
- bed_class: int32 [256, 2048], P('space'), may hold values from 0 to 15
- ice_mask: int32 [256, 2048], P('space'), may hold values 0 or 1
- zone_index: int32 [256, 2048], P('space'), may hold values from 0 to 7
- bed_levels: float32 [16], replicated, may hold values from -1 to 1
- balance_rates: float32 [8], replicated, may hold values from -0.3 to 0.3
Outputs:
- end_state: float32 [4, 256, 2048], P('tm', 'space')
- next_start: float32 [4, 256, 2048], P('tm', 'space')
All inputs are finite; a program needn't handle non-finite values. No bound on the sum of `ice_mask` on one device may be relied on, other than what follows from the above.
Results may differ from a plain program's by a relative error of at most 0.0001.
Values sent between devices are 32-bit elements; how exact they have to be, the bound alone decides.
A program may use at most 128 MiB of HBM per device.

v0:
```python
import functools

import jax
import jax.numpy as jnp
from jax import lax
from jax.experimental import pallas as pl
from jax.experimental.pallas import tpu as pltpu
from jax.sharding import PartitionSpec as P

FSTEPS = 4
CSTEPS = 2
SUB = 8
LANE = 128
BLOCK = 8

glen_factor = 0.5
diff_cap = 1.0
time_step = 0.2

MESH = pl.DeviceIdType.MESH


def load(ref, start, count):
    width = ref.shape[-1]
    return [ref[pl.ds(start, count), :, v * LANE : (v + 1) * LANE] for v in range(width // LANE)]


def store(ref, start, parts):
    for v, part in enumerate(parts):
        ref[pl.ds(start, part.shape[0]), :, v * LANE : (v + 1) * LANE] = part


def zero_rows(ref, start, count):
    ref[start : start + count] = jnp.zeros((count,) + ref.shape[1:], ref.dtype)


def lanes_of(x):
    return lax.broadcasted_iota(jnp.int32, x.shape, 2)


def subs_of(x):
    return lax.broadcasted_iota(jnp.int32, x.shape, 1)


def col_prev(parts, by):
    rolled = [pltpu.roll(x, by, 2) for x in parts]
    out = []
    for v, x in enumerate(rolled):
        if v:
            carried = rolled[v - 1]
        else:
            carried = jnp.where(subs_of(x) == 0, 0.0, pltpu.roll(rolled[-1], 1, 1))
        out.append(jnp.where(lanes_of(x) < by, carried, x))
    return out


def col_next(parts, by):
    rolled = [pltpu.roll(x, LANE - by, 2) for x in parts]
    out = []
    for v, x in enumerate(rolled):
        if v + 1 < len(rolled):
            carried = rolled[v + 1]
        else:
            carried = jnp.where(subs_of(x) == SUB - 1, 0.0, pltpu.roll(rolled[0], SUB - 1, 1))
        out.append(jnp.where(lanes_of(x) >= LANE - by, carried, x))
    return out


def each(fn, *lists):
    return [fn(*items) for items in zip(*lists)]


def flow_block(h, g, cover, gain, by, spacing, tau):
    slope_scale = glen_factor / (4.0 * spacing * spacing)
    flux_scale = tau * 0.5 / (spacing * spacing)
    s = each(jnp.add, g, h)
    mid = [x[1:-1] for x in s]
    right, left = col_next(mid, by), col_prev(mid, by)
    diffusion = []
    for x, r, l, thick in zip(s, right, left, h):
        dx = x[2:] - x[:-2]
        dy = r - l
        inner = thick[1:-1]
        square = inner * inner
        fifth = square * square * inner
        diffusion.append(jnp.minimum((slope_scale * fifth) * (dx * dx + dy * dy), diff_cap))
    centre = [d[1:-1] for d in diffusion]
    d_right, d_left = col_next(centre, by), col_prev(centre, by)
    out = []
    for v in range(len(h)):
        level, d = mid[v], diffusion[v]
        flux_x = (d[1:] + d[:-1]) * (level[1:] - level[:-1])
        here = level[1:-1]
        up = (centre[v] + d_right[v]) * (right[v][1:-1] - here)
        down = (d_left[v] + centre[v]) * (here - left[v][1:-1])
        spread = (flux_x[1:] - flux_x[:-1]) + (up - down)
        updated = h[v][2:-2] + (flux_scale * spread + gain[v])
        out.append(jnp.maximum(updated, 0.0) * cover[v])
    return out


def sweep(src, dst, ground, cover, gain, margin, by, spacing, tau):
    total = src.shape[0]
    first, last = margin, total - margin

    def block(start, count):
        h = load(src, start - 2, count + 4)
        g = load(ground, start - 2, count + 4)
        c = load(cover, start, count)
        a = load(gain, start, count)
        store(dst, start, flow_block(h, g, c, a, by, spacing, tau))

    blocks, rest = divmod(last - first, BLOCK)

    def body(i, carry):
        block(first + i * BLOCK, BLOCK)
        return carry

    lax.fori_loop(0, blocks, body, 0)
    if rest:
        block(first + blocks * BLOCK, rest)


def lookup(index, table_ref):
    values = [table_ref[i] for i in range(table_ref.shape[0])]
    bit = 1
    while len(values) > 1:
        mask = (index & bit) != 0
        if len(values) % 2:
            values.append(values[-1])
        values = [jnp.where(mask, values[i + 1], values[i]) for i in range(0, len(values), 2)]
        bit *= 2
    return values[0]


def restrict(parts):
    out = []
    for x in parts:
        pairs = x.reshape((x.shape[0] // 2, 2) + x.shape[1:])
        y = pairs[:, 0] + pairs[:, 1]
        even = (lanes_of(y) & 1) == 0
        out.append((y + jnp.where(even, pltpu.roll(y, LANE - 1, 2), pltpu.roll(y, 1, 2))) * 0.25)
    return out


def prolong(parts):
    out = []
    for x in parts:
        twice = jnp.broadcast_to(x[:, None], (x.shape[0], 2) + x.shape[1:])
        out.append(twice.reshape((2 * x.shape[0],) + x.shape[1:]))
    return out


def pack(parts):
    out = []
    for x in parts:
        pairs = x.reshape((x.shape[0] // 2, 2) + x.shape[1:])
        top, low = pairs[:, 0], pairs[:, 1]
        out.append(jnp.where((lanes_of(top) & 1) == 0, top, low))
    return out


def unpack(parts):
    out = []
    for x in parts:
        even = (lanes_of(x) & 1) == 0
        top = jnp.where(even, x, pltpu.roll(x, 1, 2))
        low = jnp.where(even, pltpu.roll(x, LANE - 1, 2), x)
        both = jnp.concatenate([top[:, None], low[:, None]], axis=1)
        out.append(both.reshape((2 * x.shape[0],) + x.shape[1:]))
    return out


def kernel(
    thick_hbm, bed_hbm, ice_hbm, zone_hbm, levels_ref, rates_ref,
    end_hbm, next_hbm,
    ha, hb, hc, bedx, icex, zonex, ground, cover, gain,
    cga, cgb, prev, jump, cground, ccover, cgain,
    packed_in, packed_out, prev_end, end_buf, next_buf,
    load_sem, halo_send, halo_recv, chain_send, chain_recv, end_send, end_recv, out_sem,
):
    t, s = lax.axis_index("tm"), lax.axis_index("space")
    n_t, n_s = lax.axis_size("tm"), lax.axis_size("space")
    fh = 2 * FSTEPS
    ch = 2 * CSTEPS
    rows = thick_hbm.shape[1]
    width = ha.shape[2]
    crows = rows // 2
    coarse_tau = time_step * FSTEPS / CSTEPS

    has_up, has_low = s > 0, s < n_s - 1
    has_prev, has_next = t > 0, t < n_t - 1

    sources = (thick_hbm.at[0], bed_hbm, ice_hbm, zone_hbm)
    fields = (ha, bedx, icex, zonex)
    loads = []
    for f, (src, dst) in enumerate(zip(sources, fields)):
        for k in range(SUB):
            cp = pltpu.make_async_copy(
                src.at[:, k * width : (k + 1) * width], dst.at[fh : fh + rows, k, :], load_sem.at[f, k]
            )
            cp.start()
            loads.append(cp)

    partners = [
        (has_up, (t, s - 1)),
        (has_low, (t, s + 1)),
        (has_prev, (t - 1, s)),
        (has_next, (t + 1, s)),
        (has_prev & has_up, (t - 1, s - 1)),
        (has_prev & has_low, (t - 1, s + 1)),
        (has_next & has_up, (t + 1, s - 1)),
        (has_next & has_low, (t + 1, s + 1)),
    ]
    barrier = pltpu.get_barrier_semaphore()
    for cond, device in partners:
        @pl.when(cond)
        def _(device=device):
            pl.semaphore_signal(barrier, inc=1, device_id=device, device_id_type=MESH)
    sides = has_up.astype(jnp.int32) + has_low.astype(jnp.int32)
    slices = has_prev.astype(jnp.int32) + has_next.astype(jnp.int32)
    pl.semaphore_wait(barrier, sides + slices * (1 + sides))

    for cp in loads:
        cp.wait()

    def remote(src, dst, ssem, rsem, device):
        return pltpu.make_async_remote_copy(
            src_ref=src, dst_ref=dst, send_sem=ssem, recv_sem=rsem, device_id=device, device_id_type=MESH
        )

    def halo_copy(side, f):
        ref = fields[f]
        if side == 0:
            src, dst, device = ref.at[fh : 2 * fh], ref.at[fh + rows : 2 * fh + rows], (t, s - 1)
        else:
            src, dst, device = ref.at[rows : fh + rows], ref.at[0:fh], (t, s + 1)
        return remote(src, dst, halo_send.at[side, f], halo_recv.at[side, f], device)

    for side, cond in ((0, has_up), (1, has_low)):
        @pl.when(cond)
        def _(side=side):
            for f in range(len(fields)):
                halo_copy(side, f).start()

    def look_rows(start, count):
        store(ground, start, [lookup(x, levels_ref) for x in load(bedx, start, count)])
        store(gain, start, [time_step * lookup(x, rates_ref) for x in load(zonex, start, count)])
        store(cover, start, [x.astype(jnp.float32) for x in load(icex, start, count)])

    def coarsen(start, count):
        half, n = start // 2 if isinstance(start, int) else lax.div(start, 2), count // 2
        store(cground, half, restrict(load(ground, start, count)))
        store(ccover, half, restrict(load(cover, start, count)))
        store(cgain, half, [x * (coarse_tau / time_step) for x in restrict(load(gain, start, count))])
        store(cga, half, restrict(load(ha, start, count)))

    def own_rows(i, carry):
        start = fh + i * 8
        look_rows(start, 8)
        coarsen(start, 8)
        return carry

    lax.fori_loop(0, rows // 8, own_rows, 0)

    for side, cond, start in ((1, has_up, 0), (0, has_low, fh + rows)):
        @pl.when(cond)
        def _(side=side, start=start):
            for f in range(len(fields)):
                halo_copy(side, f).wait_recv()
            look_rows(start, fh)

        @pl.when(jnp.logical_not(cond))
        def _(start=start):
            for ref in (ha, ground, cover, gain):
                zero_rows(ref, start, fh)

        coarsen(start, fh)

    chain = (ha, hb, hc, hb, hc)
    for step in range(FSTEPS):
        sweep(chain[step], chain[step + 1], ground, cover, gain, 2 * (step + 1), 1, 1.0, time_step)
    fine = hc

    def end_copy():
        return remote(fine.at[fh : fh + rows], prev_end, end_send.at[0], end_recv.at[0], (t + 1, s))

    def chain_copy(part, slot):
        n, m = ch // 2, crows // 2
        src = (packed_out, packed_out.at[0:n], packed_out.at[m - n : m])[part]
        low, high = ((n, n + m), (n + m, 2 * n + m), (0, n))[part]
        dst = packed_in.at[low:high]
        return remote(src, dst, chain_send.at[part], chain_recv.at[part], (slot, (s, s - 1, s + 1)[part]))

    chain_conds = (has_next, has_next & has_up, has_next & has_low)

    def coarse_run(src, tmp, dst):
        sweep(src, tmp, cground, ccover, cgain, 2, 2, 2.0, coarse_tau)
        sweep(tmp, dst, cground, ccover, cgain, 4, 2, 2.0, coarse_tau)

    coarse_run(cga, cgb, prev)

    def jump_rows(i, carry):
        fine_mean = restrict(load(fine, fh + 8 * i, 8))
        store(jump, ch + 4 * i, each(jnp.subtract, fine_mean, load(prev, ch + 4 * i, 4)))
        return carry

    lax.fori_loop(0, rows // 8, jump_rows, 0)

    @pl.when(has_next & has_prev)
    def _():
        end_copy().start()

    @pl.when(has_prev)
    def _():
        n, m = ch // 2, crows // 2
        chain_copy(0, t - 1).wait_recv()
        store(cga, ch, unpack(load(packed_in, n, m)))

        @pl.when(has_low)
        def _():
            chain_copy(1, t - 1).wait_recv()
            store(cga, ch + crows, unpack(load(packed_in, n + m, n)))

        @pl.when(has_up)
        def _():
            chain_copy(2, t - 1).wait_recv()
            store(cga, 0, unpack(load(packed_in, 0, n)))

        @pl.when(jnp.logical_not(has_low))
        def _():
            zero_rows(cga, ch + crows, ch)

        @pl.when(jnp.logical_not(has_up))
        def _():
            zero_rows(cga, 0, ch)

        coarse_run(cga, cgb, prev)

    def current_rows(i, carry):
        row = ch + 4 * i
        value = each(jnp.add, load(prev, row, 4), load(jump, row, 4))
        store(cgb, row, value)
        store(packed_out, 2 * i, pack(value))
        return carry

    lax.fori_loop(0, crows // 4, current_rows, 0)

    for part, cond in enumerate(chain_conds):
        @pl.when(cond)
        def _(part=part):
            chain_copy(part, t + 1).start()

    @pl.when(has_next & jnp.logical_not(has_prev))
    def _():
        end_copy().start()

    def finish(fine_ref, fine_at, current_ref, out_ref):
        def body(i, carry):
            e = load(fine_ref, fine_at + 8 * i, 8)
            diff = each(jnp.subtract, load(current_ref, ch + 4 * i, 4), restrict(e))
            store(out_ref, 8 * i, each(jnp.add, e, prolong(diff)))
            return carry

        lax.fori_loop(0, rows // 8, body, 0)

    def write_out(buf, at, out, slot):
        return [
            pltpu.make_async_copy(
                buf.at[at : at + rows, k, :], out.at[0, :, k * width : (k + 1) * width], out_sem.at[slot, k]
            )
            for k in range(SUB)
        ]

    finish(fine, fh, cgb, end_buf)
    end_writes = write_out(end_buf, 0, end_hbm, 0)
    for cp in end_writes:
        cp.start()

    @pl.when(has_prev)
    def _():
        remote(fine.at[fh : fh + rows], prev_end, end_send.at[0], end_recv.at[0], (t - 1, s)).wait_recv()
        finish(prev_end, 0, cga, next_buf)

    @pl.when(jnp.logical_not(has_prev))
    def _():
        next_buf[...] = ha[fh : fh + rows]

    next_writes = write_out(next_buf, 0, next_hbm, 1)
    for cp in next_writes:
        cp.start()

    for side, cond in ((0, has_up), (1, has_low)):
        @pl.when(cond)
        def _(side=side):
            for f in range(len(fields)):
                halo_copy(side, f).wait_send()
    for part, cond in enumerate(chain_conds):
        @pl.when(cond)
        def _(part=part):
            chain_copy(part, t + 1).wait_send()

    @pl.when(has_next)
    def _():
        end_copy().wait_send()

    for cp in end_writes + next_writes:
        cp.wait()


def per_device(thickness, bed_class, ice_mask, zone_index, bed_levels, balance_rates):
    _, rows, cols = thickness.shape
    width = cols // SUB
    crows = rows // 2
    fx, cx = rows + 4 * FSTEPS, crows + 4 * CSTEPS

    def buf(count, dtype=jnp.float32):
        return pltpu.VMEM((count, SUB, width), dtype)

    dma = pltpu.SemaphoreType.DMA
    shape = jax.ShapeDtypeStruct(thickness.shape, jnp.float32)
    return pl.pallas_call(
        kernel,
        out_shape=(shape, shape),
        in_specs=[pl.BlockSpec(memory_space=pl.ANY)] * 4 + [pl.BlockSpec(memory_space=pltpu.SMEM)] * 2,
        out_specs=(pl.BlockSpec(memory_space=pl.ANY), pl.BlockSpec(memory_space=pl.ANY)),
        scratch_shapes=[
            buf(fx), buf(fx), buf(fx),
            buf(fx, jnp.int32), buf(fx, jnp.int32), buf(fx, jnp.int32),
            buf(fx), buf(fx), buf(fx),
            buf(cx), buf(cx), buf(cx), buf(cx), buf(cx), buf(cx), buf(cx),
            buf(cx // 2), buf(crows // 2), buf(rows), buf(rows), buf(rows),
            dma((4, SUB)), dma((2, 4)), dma((2, 4)), dma((3,)), dma((3,)), dma((1,)), dma((1,)), dma((2, SUB)),
        ],
        compiler_params=pltpu.CompilerParams(collective_id=0, has_side_effects=True),
    )(thickness, bed_class, ice_mask, zone_index, bed_levels, balance_rates)


def solution(mesh):
    placed = (
        P("tm", "space", None),
        P("space", None),
        P("space", None),
        P("space", None),
        P(),
        P(),
    )
    return jax.shard_map(
        per_device,
        mesh=mesh,
        in_specs=placed,
        out_specs=(P("tm", "space", None), P("tm", "space", None)),
        check_vma=False,
    )
```

profile of v0, /device:TPU:28, one launch (start us, length us, event | category | flops | bytes accessed | tf_op | source)
XLA Modules:
  0.0 38.5 jit_solution(2215294370425259266)
XLA Ops:
  0.6 35.5 %shard_map.77 = (f32[1,32,2048]{2,1,0:T(8,128)}, f32[1,32,2048]{2,1,0:T(8,128)}) custom-call(f32[1,32,2048]{2,1,0:T(8,128)} %thick_hbm.1, s32[32,2048]{1,0:T(8,128)} %bed_hbm.1, s32[32,2048]{1,0:T(8,128)} %ice_hbm.1, s32[32,2048]{1,0:T(8,128)} %zone_hbm.1, f32[16]{0:T(128)} %levels_ref.1, f32[8]{0:T(128)} %rates_ref.1), custom_call_target="tpu_custom_call" | custom-call | tf_op jit(solution)/shard_map/pallas_call | solution.py:422
  36.1 0.0 copy-start
  36.1 1.7 %copy.10 = f32[1,32,2048]{2,1,0:T(8,128)} copy(f32[1,32,2048]{2,1,0:T(8,128)} %get-tuple-element.4) | data formatting | bytes 524288
  37.8 0.0 copy-done
  37.8 0.7 %copy.11 = f32[1,32,2048]{2,1,0:T(8,128)} copy(f32[1,32,2048]{2,1,0:T(8,128)S(1)} %copy-done) | data formatting | bytes 524288
Async XLA Ops:
  36.1 1.7 %copy-start = (f32[1,32,2048]{2,1,0:T(8,128)S(1)}, f32[1,32,2048]{2,1,0:T(8,128)}, u32[]{:S(2)}) copy-start(f32[1,32,2048]{2,1,0:T(8,128)} %get-tuple-element.5) | copy-start | bytes 786436
where the time goes:
time: 38.7 us; the launch traced here: 38.5 us
  Pallas kernels  35.5 us (92%)
  local copies, waits for them, and re-layouts  2.42 us (6%)
  between operations  0.65 us (2%)
    pallas_call x1, Pallas kernels, per_device(): pl.pallas_call(kernel, out_shape=(shape, shape), in_specs=[pl.BlockSpec(m...  35.5 us
    unnamed x4, local copies, waits for them, and re-layouts  2.42 us

commit v1 on v0

--- a/solution.py
+++ b/solution.py
@@ -99,10 +99,7 @@
     return out
 
 
-def sweep(src, dst, ground, cover, gain, margin, by, spacing, tau):
-    total = src.shape[0]
-    first, last = margin, total - margin
-
+def sweep(src, dst, ground, cover, gain, first, rows, by, spacing, tau):
     def block(start, count):
         h = load(src, start - 2, count + 4)
         g = load(ground, start - 2, count + 4)
@@ -110,13 +107,16 @@
         a = load(gain, start, count)
         store(dst, start, flow_block(h, g, c, a, by, spacing, tau))
 
-    blocks, rest = divmod(last - first, BLOCK)
+    blocks, rest = divmod(rows, BLOCK)
 
     def body(i, carry):
         block(first + i * BLOCK, BLOCK)
         return carry
 
-    lax.fori_loop(0, blocks, body, 0)
+    if blocks == 1:
+        block(first, BLOCK)
+    elif blocks:
+        lax.fori_loop(0, blocks, body, 0)
     if rest:
         block(first + blocks * BLOCK, rest)
 
@@ -229,12 +229,14 @@
             src_ref=src, dst_ref=dst, send_sem=ssem, recv_sem=rsem, device_id=device, device_id_type=MESH
         )
 
+    depth = (fh, fh, fh - 2, fh - 2)
+
     def halo_copy(side, f):
-        ref = fields[f]
+        ref, n = fields[f], depth[f]
         if side == 0:
-            src, dst, device = ref.at[fh : 2 * fh], ref.at[fh + rows : 2 * fh + rows], (t, s - 1)
+            src, dst, device = ref.at[fh : fh + n], ref.at[fh + rows : fh + rows + n], (t, s - 1)
         else:
-            src, dst, device = ref.at[rows : fh + rows], ref.at[0:fh], (t, s + 1)
+            src, dst, device = ref.at[fh + rows - n : fh + rows], ref.at[fh - n : fh], (t, s + 1)
         return remote(src, dst, halo_send.at[side, f], halo_recv.at[side, f], device)
 
     for side, cond in ((0, has_up), (1, has_low)):
@@ -249,11 +251,24 @@
         store(cover, start, [x.astype(jnp.float32) for x in load(icex, start, count)])
 
     def coarsen(start, count):
-        half, n = start // 2 if isinstance(start, int) else lax.div(start, 2), count // 2
+        half = start // 2 if isinstance(start, int) else lax.div(start, 2)
         store(cground, half, restrict(load(ground, start, count)))
         store(ccover, half, restrict(load(cover, start, count)))
         store(cgain, half, [x * (coarse_tau / time_step) for x in restrict(load(gain, start, count))])
         store(cga, half, restrict(load(ha, start, count)))
+
+    chain = (ha, hb, hc, hb, hc)
+    fine = hc
+
+    def fine_sweep(step, first, count):
+        sweep(chain[step], chain[step + 1], ground, cover, gain, first, count, 1, 1.0, time_step)
+
+    def coarse_sweep(src, dst, first, count):
+        sweep(src, dst, cground, ccover, cgain, first, count, 2, 2.0, coarse_tau)
+
+    def jump_rows(row, count):
+        fine_mean = restrict(load(fine, 2 * row, 2 * count))
+        store(jump, row, each(jnp.subtract, fine_mean, load(prev, row, count)))
 
     def own_rows(i, carry):
         start = fh + i * 8
@@ -263,24 +278,47 @@
 
     lax.fori_loop(0, rows // 8, own_rows, 0)
 
-    for side, cond, start in ((1, has_up, 0), (0, has_low, fh + rows)):
-        @pl.when(cond)
-        def _(side=side, start=start):
+    for step in range(FSTEPS):
+        edge = 2 * (step + 1)
+        fine_sweep(step, fh + edge, rows - 2 * edge)
+    coarse_sweep(cga, cgb, ch + 2, crows - 4)
+    coarse_sweep(cgb, prev, ch + 4, crows - 8)
+    jump_rows(2 * ch, crows - 2 * ch)
+
+    def one_side(j, carry):
+        side = lax.rem(s + j, 2)
+        upper = side == 1
+
+        def pick(up, low):
+            return jnp.where(upper, up, low)
+
+        start = pick(0, fh + rows)
+        there = (upper & has_up) | (jnp.logical_not(upper) & has_low)
+
+        @pl.when(there)
+        def _():
             for f in range(len(fields)):
-                halo_copy(side, f).wait_recv()
+                n = depth[f]
+                ref = fields[f].at[pl.ds(pick(fh - n, fh + rows), n)]
+                remote(ref, ref, halo_send.at[side, f], halo_recv.at[side, f], (t, pick(s - 1, s + 1))).wait_recv()
             look_rows(start, fh)
 
-        @pl.when(jnp.logical_not(cond))
-        def _(start=start):
+        @pl.when(jnp.logical_not(there))
+        def _():
             for ref in (ha, ground, cover, gain):
-                zero_rows(ref, start, fh)
+                zero = jnp.zeros((fh, SUB, LANE), ref.dtype)
+                store(ref, start, [zero] * (width // LANE))
 
         coarsen(start, fh)
-
-    chain = (ha, hb, hc, hb, hc)
-    for step in range(FSTEPS):
-        sweep(chain[step], chain[step + 1], ground, cover, gain, 2 * (step + 1), 1, 1.0, time_step)
-    fine = hc
+        for step in range(FSTEPS):
+            edge = 2 * (step + 1)
+            fine_sweep(step, pick(edge, fh + rows - edge), fh)
+        coarse_sweep(cga, cgb, pick(2, ch + crows - 2), ch)
+        coarse_sweep(cgb, prev, pick(4, ch + crows - 4), ch)
+        jump_rows(pick(ch, crows), ch)
+        return carry
+
+    lax.fori_loop(0, 2, one_side, 0)
 
     def end_copy():
         return remote(fine.at[fh : fh + rows], prev_end, end_send.at[0], end_recv.at[0], (t + 1, s))
@@ -295,17 +333,8 @@
     chain_conds = (has_next, has_next & has_up, has_next & has_low)
 
     def coarse_run(src, tmp, dst):
-        sweep(src, tmp, cground, ccover, cgain, 2, 2, 2.0, coarse_tau)
-        sweep(tmp, dst, cground, ccover, cgain, 4, 2, 2.0, coarse_tau)
-
-    coarse_run(cga, cgb, prev)
-
-    def jump_rows(i, carry):
-        fine_mean = restrict(load(fine, fh + 8 * i, 8))
-        store(jump, ch + 4 * i, each(jnp.subtract, fine_mean, load(prev, ch + 4 * i, 4)))
-        return carry
-
-    lax.fori_loop(0, rows // 8, jump_rows, 0)
+        coarse_sweep(src, tmp, 2, crows + 2 * ch - 4)
+        coarse_sweep(tmp, dst, ch, crows)
 
     @pl.when(has_next & has_prev)
     def _():

time: 38.7 us -> 32.9 us (0.85)
  Pallas kernels: 35.5 us -> 29.7 us
    pallas_call x1, Pallas kernels: 35.5 us -> 29.7 us  [per_device(): pl.pallas_call(kernel, out_shape=(shape, shape), in_specs=[pl.BlockSpec(m...]
where the time goes in v1:
time: 32.9 us; the launch traced here: 32.7 us
  Pallas kernels  29.7 us (90%)
  local copies, waits for them, and re-layouts  2.42 us (7%)
  between operations  0.65 us (2%)
    pallas_call x1, Pallas kernels, per_device(): pl.pallas_call(kernel, out_shape=(shape, shape), in_specs=[pl.BlockSpec(m...  29.7 us
    unnamed x4, local copies, waits for them, and re-layouts  2.42 us

profile of v1, /device:TPU:28, one launch (start us, length us, event | category | flops | bytes accessed | tf_op | source)
XLA Modules:
  0.0 32.7 jit_solution(18166790605458601296)
XLA Ops:
  0.6 29.7 %shard_map.77 = (f32[1,32,2048]{2,1,0:T(8,128)}, f32[1,32,2048]{2,1,0:T(8,128)}) custom-call(f32[1,32,2048]{2,1,0:T(8,128)} %thick_hbm.1, s32[32,2048]{1,0:T(8,128)} %bed_hbm.1, s32[32,2048]{1,0:T(8,128)} %ice_hbm.1, s32[32,2048]{1,0:T(8,128)} %zone_hbm.1, f32[16]{0:T(128)} %levels_ref.1, f32[8]{0:T(128)} %rates_ref.1), custom_call_target="tpu_custom_call" | custom-call | tf_op jit(solution)/shard_map/pallas_call | solution.py:451
  30.3 0.0 copy-start
  30.3 1.7 %copy.10 = f32[1,32,2048]{2,1,0:T(8,128)} copy(f32[1,32,2048]{2,1,0:T(8,128)} %get-tuple-element.4) | data formatting | bytes 524288
  32.0 0.0 copy-done
  32.0 0.7 %copy.11 = f32[1,32,2048]{2,1,0:T(8,128)} copy(f32[1,32,2048]{2,1,0:T(8,128)S(1)} %copy-done) | data formatting | bytes 524288
Async XLA Ops:
  30.3 1.7 %copy-start = (f32[1,32,2048]{2,1,0:T(8,128)S(1)}, f32[1,32,2048]{2,1,0:T(8,128)}, u32[]{:S(2)}) copy-start(f32[1,32,2048]{2,1,0:T(8,128)} %get-tuple-element.5) | copy-start | bytes 786436

commit v2 on v1

--- a/solution.py
+++ b/solution.py
@@ -151,24 +151,20 @@
     return out
 
 
-def pack(parts):
-    out = []
-    for x in parts:
-        pairs = x.reshape((x.shape[0] // 2, 2) + x.shape[1:])
-        top, low = pairs[:, 0], pairs[:, 1]
-        out.append(jnp.where((lanes_of(top) & 1) == 0, top, low))
-    return out
-
-
-def unpack(parts):
-    out = []
-    for x in parts:
-        even = (lanes_of(x) & 1) == 0
-        top = jnp.where(even, x, pltpu.roll(x, 1, 2))
-        low = jnp.where(even, pltpu.roll(x, LANE - 1, 2), x)
-        both = jnp.concatenate([top[:, None], low[:, None]], axis=1)
-        out.append(both.reshape((2 * x.shape[0],) + x.shape[1:]))
-    return out
+def is_even(x):
+    return (lanes_of(x) & 1) == 0
+
+
+def to_odd(x):
+    return pltpu.roll(x, 1, 2)
+
+
+def to_even(x):
+    return pltpu.roll(x, LANE - 1, 2)
+
+
+def merge(evens, odds):
+    return [jnp.where(is_even(x), x, y) for x, y in zip(evens, odds)]
 
 
 def kernel(
@@ -176,8 +172,8 @@
     end_hbm, next_hbm,
     ha, hb, hc, bedx, icex, zonex, ground, cover, gain,
     cga, cgb, prev, jump, cground, ccover, cgain,
-    packed_in, packed_out, prev_end, end_buf, next_buf,
-    load_sem, halo_send, halo_recv, chain_send, chain_recv, end_send, end_recv, out_sem,
+    pground, pcover, pgain, pjump, pcur, ptmp, pout, edge_out, edge_in, prev_end, end_buf, next_buf,
+    load_sem, halo_send, halo_recv, chain_send, chain_recv, end_send, end_recv, out_sem, ready_sem,
 ):
     t, s = lax.axis_index("tm"), lax.axis_index("space")
     n_t, n_s = lax.axis_size("tm"), lax.axis_size("space")
@@ -186,6 +182,8 @@
     rows = thick_hbm.shape[1]
     width = ha.shape[2]
     crows = rows // 2
+    half = crows // 2
+    edge_rows = CSTEPS
     coarse_tau = time_step * FSTEPS / CSTEPS
 
     has_up, has_low = s > 0, s < n_s - 1
@@ -207,10 +205,6 @@
         (has_low, (t, s + 1)),
         (has_prev, (t - 1, s)),
         (has_next, (t + 1, s)),
-        (has_prev & has_up, (t - 1, s - 1)),
-        (has_prev & has_low, (t - 1, s + 1)),
-        (has_next & has_up, (t + 1, s - 1)),
-        (has_next & has_low, (t + 1, s + 1)),
     ]
     barrier = pltpu.get_barrier_semaphore()
     for cond, device in partners:
@@ -219,7 +213,11 @@
             pl.semaphore_signal(barrier, inc=1, device_id=device, device_id_type=MESH)
     sides = has_up.astype(jnp.int32) + has_low.astype(jnp.int32)
     slices = has_prev.astype(jnp.int32) + has_next.astype(jnp.int32)
-    pl.semaphore_wait(barrier, sides + slices * (1 + sides))
+    pl.semaphore_wait(barrier, sides + slices)
+
+    @pl.when(has_prev)
+    def _():
+        pl.semaphore_signal(ready_sem, inc=1, device_id=(t - 1, s), device_id_type=MESH)
 
     for cp in loads:
         cp.wait()
@@ -270,6 +268,14 @@
         fine_mean = restrict(load(fine, 2 * row, 2 * count))
         store(jump, row, each(jnp.subtract, fine_mean, load(prev, row, count)))
 
+    def end_copy(piece, start, count, slot):
+        return remote(
+            fine.at[pl.ds(fh + start, count)], prev_end.at[pl.ds(start, count)],
+            end_send.at[piece], end_recv.at[piece], (slot, s),
+        )
+
+    end_pieces = ((0, fh, rows - 2 * fh), (1, rows - fh, fh), (2, 0, fh))
+
     def own_rows(i, carry):
         start = fh + i * 8
         look_rows(start, 8)
@@ -281,6 +287,11 @@
     for step in range(FSTEPS):
         edge = 2 * (step + 1)
         fine_sweep(step, fh + edge, rows - 2 * edge)
+
+    @pl.when(has_next)
+    def _():
+        end_copy(*end_pieces[0], t + 1).start()
+
     coarse_sweep(cga, cgb, ch + 2, crows - 4)
     coarse_sweep(cgb, prev, ch + 4, crows - 8)
     jump_rows(2 * ch, crows - 2 * ch)
@@ -313,6 +324,11 @@
         for step in range(FSTEPS):
             edge = 2 * (step + 1)
             fine_sweep(step, pick(edge, fh + rows - edge), fh)
+
+        @pl.when(has_next & ((j == 0) | has_prev))
+        def _():
+            end_copy(1 + side, pick(0, rows - fh), fh, t + 1).start()
+
         coarse_sweep(cga, cgb, pick(2, ch + crows - 2), ch)
         coarse_sweep(cgb, prev, pick(4, ch + crows - 4), ch)
         jump_rows(pick(ch, crows), ch)
@@ -320,78 +336,40 @@
 
     lax.fori_loop(0, 2, one_side, 0)
 
-    def end_copy():
-        return remote(fine.at[fh : fh + rows], prev_end, end_send.at[0], end_recv.at[0], (t + 1, s))
-
     def chain_copy(part, slot):
-        n, m = ch // 2, crows // 2
-        src = (packed_out, packed_out.at[0:n], packed_out.at[m - n : m])[part]
-        low, high = ((n, n + m), (n + m, 2 * n + m), (0, n))[part]
-        dst = packed_in.at[low:high]
+        src = (pout, edge_out.at[0], edge_out.at[1])[part]
+        dst = (pcur.at[ch : ch + half], edge_in.at[0], edge_in.at[1])[part]
         return remote(src, dst, chain_send.at[part], chain_recv.at[part], (slot, (s, s - 1, s + 1)[part]))
 
     chain_conds = (has_next, has_next & has_up, has_next & has_low)
 
-    def coarse_run(src, tmp, dst):
-        coarse_sweep(src, tmp, 2, crows + 2 * ch - 4)
-        coarse_sweep(tmp, dst, ch, crows)
-
-    @pl.when(has_next & has_prev)
-    def _():
-        end_copy().start()
+    def packed_rows(ref, row, count):
+        return merge(load(ref, row, count), load(ref, row + half, count))
+
+    store(pjump, 0, packed_rows(jump, ch, half))
+
+    @pl.when(jnp.logical_not(has_prev))
+    def _():
+        store(ptmp, ch, packed_rows(prev, ch, half))
 
     @pl.when(has_prev)
     def _():
-        n, m = ch // 2, crows // 2
-        chain_copy(0, t - 1).wait_recv()
-        store(cga, ch, unpack(load(packed_in, n, m)))
-
-        @pl.when(has_low)
-        def _():
-            chain_copy(1, t - 1).wait_recv()
-            store(cga, ch + crows, unpack(load(packed_in, n + m, n)))
-
-        @pl.when(has_up)
-        def _():
-            chain_copy(2, t - 1).wait_recv()
-            store(cga, 0, unpack(load(packed_in, 0, n)))
-
-        @pl.when(jnp.logical_not(has_low))
-        def _():
-            zero_rows(cga, ch + crows, ch)
-
-        @pl.when(jnp.logical_not(has_up))
-        def _():
-            zero_rows(cga, 0, ch)
-
-        coarse_run(cga, cgb, prev)
-
-    def current_rows(i, carry):
-        row = ch + 4 * i
-        value = each(jnp.add, load(prev, row, 4), load(jump, row, 4))
-        store(cgb, row, value)
-        store(packed_out, 2 * i, pack(value))
-        return carry
-
-    lax.fori_loop(0, crows // 4, current_rows, 0)
-
-    for part, cond in enumerate(chain_conds):
-        @pl.when(cond)
-        def _(part=part):
-            chain_copy(part, t + 1).start()
-
-    @pl.when(has_next & jnp.logical_not(has_prev))
-    def _():
-        end_copy().start()
-
-    def finish(fine_ref, fine_at, current_ref, out_ref):
+        for src, dst in ((cground, pground), (ccover, pcover), (cgain, pgain)):
+            store(dst, 0, packed_rows(src, 0, half))
+            store(dst, half, packed_rows(src, half, 2 * ch))
+
+    def finish(fine_ref, fine_at, current_ref, current_at, out_ref):
         def body(i, carry):
-            e = load(fine_ref, fine_at + 8 * i, 8)
-            diff = each(jnp.subtract, load(current_ref, ch + 4 * i, 4), restrict(e))
-            store(out_ref, 8 * i, each(jnp.add, e, prolong(diff)))
+            p = load(current_ref, current_at + 4 * i, 4)
+            top = merge(p, [to_odd(x) for x in p])
+            low = merge([to_even(x) for x in p], p)
+            for current, at in ((top, 8 * i), (low, 2 * half + 8 * i)):
+                e = load(fine_ref, fine_at + at, 8)
+                diff = each(jnp.subtract, current, restrict(e))
+                store(out_ref, at, each(jnp.add, e, prolong(diff)))
             return carry
 
-        lax.fori_loop(0, rows // 8, body, 0)
+        lax.fori_loop(0, half // 4, body, 0)
 
     def write_out(buf, at, out, slot):
         return [
@@ -401,23 +379,79 @@
             for k in range(SUB)
         ]
 
-    finish(fine, fh, cgb, end_buf)
+    next_writes = write_out(next_buf, 0, next_hbm, 1)
+
+    def next_state():
+        @pl.when(has_prev)
+        def _():
+            for piece in end_pieces:
+                end_copy(*piece, t - 1).wait_recv()
+            finish(prev_end, 0, pcur, ch, next_buf)
+
+        @pl.when(jnp.logical_not(has_prev))
+        def _():
+            next_buf[...] = ha[fh : fh + rows]
+
+        for cp in next_writes:
+            cp.start()
+
+    @pl.when(has_prev)
+    def _():
+        for part, cond in ((1, has_low), (2, has_up)):
+            @pl.when(jnp.logical_not(cond))
+            def _(part=part):
+                edge_in[part - 1] = jnp.zeros(edge_in.shape[1:], jnp.float32)
+
+        chain_copy(0, t - 1).wait_recv()
+        for part, cond in ((1, has_low), (2, has_up)):
+            @pl.when(cond)
+            def _(part=part):
+                chain_copy(part, t - 1).wait_recv()
+
+        low, up = (load(edge_in.at[side], 0, edge_rows) for side in range(2))
+        inner = load(pcur, half, ch)
+        upper = [jnp.concatenate([x, to_even(x)], axis=0) for x in up]
+        store(pcur, 0, merge(upper, [to_odd(x) for x in inner]))
+        inner = load(pcur, ch, ch)
+        lower = [jnp.concatenate([to_odd(x), x], axis=0) for x in low]
+        store(pcur, ch + half, merge([to_even(x) for x in inner], lower))
+
+        @pl.when(jnp.logical_not(has_next))
+        def _():
+            next_state()
+
+        sweep(pcur, cgb, pground, pcover, pgain, 2, half + 2 * ch - 4, 2, 2.0, coarse_tau)
+        sweep(cgb, ptmp, pground, pcover, pgain, ch, half, 2, 2.0, coarse_tau)
+
+    value = each(jnp.add, load(ptmp, ch, half), load(pjump, 0, half))
+    store(pout, 0, value)
+    n = edge_rows
+    store(edge_out.at[0], 0, merge([x[:n] for x in value], [to_odd(x[n : 2 * n]) for x in value]))
+    store(edge_out.at[1], 0, merge([to_even(x[-2 * n : -n]) for x in value], [x[-n:] for x in value]))
+
+    @pl.when(has_next)
+    def _():
+        pl.semaphore_wait(ready_sem, 1)
+
+    for part, cond in enumerate(chain_conds):
+        @pl.when(cond)
+        def _(part=part):
+            chain_copy(part, t + 1).start()
+
+    last_side = lax.rem(s + 1, 2)
+
+    @pl.when(has_next & jnp.logical_not(has_prev))
+    def _():
+        end_copy(1 + last_side, jnp.where(last_side == 1, 0, rows - fh), fh, t + 1).start()
+
+    finish(fine, fh, pout, 0, end_buf)
     end_writes = write_out(end_buf, 0, end_hbm, 0)
     for cp in end_writes:
         cp.start()
 
-    @pl.when(has_prev)
-    def _():
-        remote(fine.at[fh : fh + rows], prev_end, end_send.at[0], end_recv.at[0], (t - 1, s)).wait_recv()
-        finish(prev_end, 0, cga, next_buf)
-
-    @pl.when(jnp.logical_not(has_prev))
-    def _():
-        next_buf[...] = ha[fh : fh + rows]
-
-    next_writes = write_out(next_buf, 0, next_hbm, 1)
-    for cp in next_writes:
-        cp.start()
+    @pl.when(has_next)
+    def _():
+        next_state()
 
     for side, cond in ((0, has_up), (1, has_low)):
         @pl.when(cond)
@@ -431,7 +465,8 @@
 
     @pl.when(has_next)
     def _():
-        end_copy().wait_send()
+        for piece in end_pieces:
+            end_copy(*piece, t + 1).wait_send()
 
     for cp in end_writes + next_writes:
         cp.wait()
@@ -441,7 +476,7 @@
     _, rows, cols = thickness.shape
     width = cols // SUB
     crows = rows // 2
-    fx, cx = rows + 4 * FSTEPS, crows + 4 * CSTEPS
+    fx, cx, px = rows + 4 * FSTEPS, crows + 4 * CSTEPS, crows // 2 + 4 * CSTEPS
 
     def buf(count, dtype=jnp.float32):
         return pltpu.VMEM((count, SUB, width), dtype)
@@ -458,8 +493,10 @@
             buf(fx, jnp.int32), buf(fx, jnp.int32), buf(fx, jnp.int32),
             buf(fx), buf(fx), buf(fx),
             buf(cx), buf(cx), buf(cx), buf(cx), buf(cx), buf(cx), buf(cx),
-            buf(cx // 2), buf(crows // 2), buf(rows), buf(rows), buf(rows),
-            dma((4, SUB)), dma((2, 4)), dma((2, 4)), dma((3,)), dma((3,)), dma((1,)), dma((1,)), dma((2, SUB)),
+            buf(px), buf(px), buf(px), buf(crows // 2), buf(px), buf(px), buf(crows // 2),
+            pltpu.VMEM((2, CSTEPS, SUB, width), jnp.float32), pltpu.VMEM((2, CSTEPS, SUB, width), jnp.float32),
+            buf(rows), buf(rows), buf(rows),
+            dma((4, SUB)), dma((2, 4)), dma((2, 4)), dma((3,)), dma((3,)), dma((3,)), dma((3,)), dma((2, SUB)), pltpu.SemaphoreType.REGULAR,
         ],
         compiler_params=pltpu.CompilerParams(collective_id=0, has_side_effects=True),
     )(thickness, bed_class, ice_mask, zone_index, bed_levels, balance_rates)

time: 32.9 us -> 30 us (0.912)
  Pallas kernels: 29.7 us -> 26.8 us
    pallas_call x1, Pallas kernels: 29.7 us -> 26.8 us  [per_device(): pl.pallas_call(kernel, out_shape=(shape, shape), in_specs=[pl.BlockSpec(m...]
where the time goes in v2:
time: 30 us; the launch traced here: 29.8 us
  Pallas kernels  26.8 us (89%)
  local copies, waits for them, and re-layouts  2.42 us (8%)
  between operations  0.65 us (2%)
    pallas_call x1, Pallas kernels, per_device(): pl.pallas_call(kernel, out_shape=(shape, shape), in_specs=[pl.BlockSpec(m...  26.8 us
    unnamed x4, local copies, waits for them, and re-layouts  2.42 us

profile of v2, /device:TPU:28, one launch (start us, length us, event | category | flops | bytes accessed | tf_op | source)
XLA Modules:
  0.0 29.8 jit_solution(6375805028690525845)
XLA Ops:
  0.6 26.8 %shard_map.77 = (f32[1,32,2048]{2,1,0:T(8,128)}, f32[1,32,2048]{2,1,0:T(8,128)}) custom-call(f32[1,32,2048]{2,1,0:T(8,128)} %thick_hbm.1, s32[32,2048]{1,0:T(8,128)} %bed_hbm.1, s32[32,2048]{1,0:T(8,128)} %ice_hbm.1, s32[32,2048]{1,0:T(8,128)} %zone_hbm.1, f32[16]{0:T(128)} %levels_ref.1, f32[8]{0:T(128)} %rates_ref.1), custom_call_target="tpu_custom_call" | custom-call | tf_op jit(solution)/shard_map/pallas_call | solution.py:486
  27.4 0.0 copy-start
  27.4 1.7 %copy.10 = f32[1,32,2048]{2,1,0:T(8,128)} copy(f32[1,32,2048]{2,1,0:T(8,128)} %get-tuple-element.4) | data formatting | bytes 524288
  29.1 0.0 copy-done
  29.1 0.7 %copy.11 = f32[1,32,2048]{2,1,0:T(8,128)} copy(f32[1,32,2048]{2,1,0:T(8,128)S(1)} %copy-done) | data formatting | bytes 524288
Async XLA Ops:
  27.4 1.7 %copy-start = (f32[1,32,2048]{2,1,0:T(8,128)S(1)}, f32[1,32,2048]{2,1,0:T(8,128)}, u32[]{:S(2)}) copy-start(f32[1,32,2048]{2,1,0:T(8,128)} %get-tuple-element.5) | copy-start | bytes 786436

commit v3 on v2

--- a/solution.py
+++ b/solution.py
@@ -433,8 +433,8 @@
     def _():
         pl.semaphore_wait(ready_sem, 1)
 
-    for part, cond in enumerate(chain_conds):
-        @pl.when(cond)
+    for part in (1, 2, 0):
+        @pl.when(chain_conds[part])
         def _(part=part):
             chain_copy(part, t + 1).start()
 

time: 30 us -> 27.9 us (0.930); the launches traced: 29.8 us -> 27.3 us
  Pallas kernels: 26.8 us -> 24.3 us
    pallas_call x1, Pallas kernels: 26.8 us -> 24.3 us  [per_device(): pl.pallas_call(kernel, out_shape=(shape, shape), in_specs=[pl.BlockSpec(m...]
where the time goes in v3:
time: 27.9 us; the launch traced here: 27.3 us
  Pallas kernels  24.3 us (87%)
  local copies, waits for them, and re-layouts  2.42 us (9%)
  between operations  0.65 us (2%)
    pallas_call x1, Pallas kernels, per_device(): pl.pallas_call(kernel, out_shape=(shape, shape), in_specs=[pl.BlockSpec(m...  24.3 us
    unnamed x4, local copies, waits for them, and re-layouts  2.42 us

profile of v3, /device:TPU:28, one launch (start us, length us, event | category | flops | bytes accessed | tf_op | source)
XLA Modules:
  0.0 27.3 jit_solution(6767108347485190756)
XLA Ops:
  0.6 24.3 %shard_map.77 = (f32[1,32,2048]{2,1,0:T(8,128)}, f32[1,32,2048]{2,1,0:T(8,128)}) custom-call(f32[1,32,2048]{2,1,0:T(8,128)} %thick_hbm.1, s32[32,2048]{1,0:T(8,128)} %bed_hbm.1, s32[32,2048]{1,0:T(8,128)} %ice_hbm.1, s32[32,2048]{1,0:T(8,128)} %zone_hbm.1, f32[16]{0:T(128)} %levels_ref.1, f32[8]{0:T(128)} %rates_ref.1), custom_call_target="tpu_custom_call" | custom-call | tf_op jit(solution)/shard_map/pallas_call | solution.py:486
  24.9 0.0 copy-start
  24.9 1.7 %copy.10 = f32[1,32,2048]{2,1,0:T(8,128)} copy(f32[1,32,2048]{2,1,0:T(8,128)} %get-tuple-element.4) | data formatting | bytes 524288
  26.6 0.0 copy-done
  26.6 0.7 %copy.11 = f32[1,32,2048]{2,1,0:T(8,128)} copy(f32[1,32,2048]{2,1,0:T(8,128)S(1)} %copy-done) | data formatting | bytes 524288
Async XLA Ops:
  24.9 1.7 %copy-start = (f32[1,32,2048]{2,1,0:T(8,128)S(1)}, f32[1,32,2048]{2,1,0:T(8,128)}, u32[]{:S(2)}) copy-start(f32[1,32,2048]{2,1,0:T(8,128)} %get-tuple-element.5) | copy-start | bytes 786436
